TPU v7x, 256 devices: a whole 4x4x8 slice. The times are simulated.
256 devices in a mesh: hid: 128 (over x, z, y), seq: 2 (over core).
Axes of the slice: x: 4, y: 4, z: 8, core: 2. Of those that a mesh axis runs over, the one named last changes fastest.
Arguments:
- pre_act: bfloat16 [1536, 32768], P(('hid', 'seq')), may hold values from -6 to 6
- butterfly: bfloat16 [128, 5, 256, 256], P('hid'), may hold values from -0.15625 to 0.15625
- low_u: bfloat16 [32768, 256], P('hid'), may hold values from -0.25 to 0.25
- low_v: bfloat16 [256, 32768], P(None, 'hid'), may hold values from -0.0625 to 0.0625
- grad_out: bfloat16 [1536, 32768], P(('hid', 'seq')), may hold values from -6 to 6
Outputs:
- output: bfloat16 [1536, 32768], P(('hid', 'seq'))
- grad_pre: bfloat16 [1536, 32768], P(('hid', 'seq'))
- grad_butterfly: float32 [128, 5, 256, 256], P('hid', None, 'seq')
- grad_low_u: float32 [32768, 256], P('hid', 'seq')
- grad_low_v: float32 [256, 32768], P('seq', 'hid')
All inputs are finite; a program needn't handle non-finite values.
Results may differ from a plain program's by a relative error of at most 0.0075.
Values may be sent and summed in bfloat16 or wider, within the bound.
A program may use at most 64 MiB of HBM per device.

v0:
```python
import math
import jax
import jax.numpy as jnp
from jax import lax
from jax.sharding import PartitionSpec as P

LEVELS = 4


def swapped(x, axis, stride):
    return lax.ppermute(x, axis, [(i, i ^ 1 << stride) for i in range(lax.axis_size(axis))])


def gelu_tanh(value):
    return jax.nn.gelu(value, approximate=True)


def reduce_latents(first, second):
    both = jnp.concatenate([first, second], axis=1)
    rows, wide = both.shape
    flat = both.reshape(rows * wide // 128, 128)
    part = lax.psum_scatter(flat, "hid", scatter_dimension=0, tiled=True)
    full = lax.all_gather(part.astype(jnp.bfloat16), "hid", axis=0, tiled=True)
    full = full.reshape(rows, wide)
    return (full[:, : wide // 2], full[:, wide // 2 :])


def inner_rows(left, right):
    return lax.dot_general(
        left, right, (((0,), (0,)), ((), ())), preferred_element_type=jnp.float32
    )


def on_device(pre_act, butterfly, low_u, low_v, grad_out):
    pre_f = pre_act.astype(jnp.float32)
    act_tok = gelu_tanh(pre_f).astype(jnp.bfloat16)
    act_rows = lax.all_to_all(act_tok, "hid", split_axis=1, concat_axis=0, tiled=True)
    partners = [act_rows]
    for level in range(LEVELS):
        partners.append(swapped(act_rows, "hid", level))
    grad_rows = lax.all_to_all(grad_out, "hid", split_axis=1, concat_axis=0, tiled=True)
    latent, dlatent = reduce_latents(
        jnp.dot(act_rows, low_u, preferred_element_type=jnp.float32),
        jnp.dot(grad_rows, low_v.T, preferred_element_type=jnp.float32),
    )
    total = jnp.dot(latent, low_v, preferred_element_type=jnp.float32)
    for level in range(LEVELS + 1):
        total = total + jnp.dot(
            partners[level], butterfly[0, level], preferred_element_type=jnp.float32
        )
    output_rows = total.astype(jnp.bfloat16)
    output_tok = lax.all_to_all(output_rows, "hid", split_axis=0, concat_axis=1, tiled=True)
    backward = jnp.dot(dlatent, low_u.T, preferred_element_type=jnp.float32)
    backward = backward + jnp.dot(grad_rows, butterfly[0, 0].T, preferred_element_type=jnp.float32)
    for level in range(1, LEVELS + 1):
        grad_far, weight_far = swapped((grad_rows, butterfly[0, level]), "hid", level - 1)
        backward = backward + jnp.dot(grad_far, weight_far.T, preferred_element_type=jnp.float32)
    grad_act = backward.astype(jnp.bfloat16)
    tokens_all = pre_act.shape[0] * lax.axis_size("hid") * lax.axis_size("seq")
    factor = 1.0 / math.sqrt(tokens_all)
    block_grads = jnp.stack(
        [inner_rows(partners[level], grad_rows) for level in range(LEVELS + 1)], axis=0
    )
    block_grads = block_grads[None] * factor
    low_u_grad = inner_rows(act_rows, dlatent) * factor
    low_v_grad = inner_rows(latent, grad_rows) * factor
    grad_butterfly, grad_low_u, grad_low_v = (
        lax.psum_scatter(
            block_grads.astype(jnp.bfloat16), "seq", scatter_dimension=2, tiled=True
        ).astype(jnp.float32),
        lax.psum_scatter(
            low_u_grad.astype(jnp.bfloat16), "seq", scatter_dimension=1, tiled=True
        ).astype(jnp.float32),
        lax.psum_scatter(
            low_v_grad.astype(jnp.bfloat16), "seq", scatter_dimension=0, tiled=True
        ).astype(jnp.float32),
    )
    grad_act_tok = lax.all_to_all(grad_act, "hid", split_axis=0, concat_axis=1, tiled=True)
    unused, pullback = jax.vjp(gelu_tanh, pre_f)
    grad_pre = pullback(grad_act_tok.astype(jnp.float32))[0].astype(jnp.bfloat16)
    return (output_tok, grad_pre, grad_butterfly, grad_low_u, grad_low_v)


def solution(mesh):
    in_specs = (
        P(("hid", "seq"), None),
        P("hid", None, None, None),
        P("hid", None),
        P(None, "hid"),
        P(("hid", "seq"), None),
    )
    out_specs = (
        P(("hid", "seq"), None),
        P(("hid", "seq"), None),
        P("hid", None, "seq", None),
        P("hid", "seq"),
        P("seq", "hid"),
    )
    return jax.shard_map(
        on_device, mesh=mesh, in_specs=in_specs, out_specs=out_specs, check_vma=False
    )
```

profile of v0, /device:TPU:32, one launch (start us, length us, event | category | flops | bytes accessed | tf_op | source)
XLA Modules:
  0.0 1346.6 jit_solution(5480149929187112660)
XLA Ops:
  7.2 1.4 fusion.22
  8.6 33.9 %all_to_all.70 = bf16[6,128,256]{2,0,1:T(8,128)(2,1)S(1)} all-to-all(bf16[6,128,256]{2,0,1:T(8,128)(2,1)S(1)} %bitcast.92), channel_id=1, replica_groups=mesh['hid'=128,'seq'=2] {'hid'}, dimensions={1} | all-to-all | bytes 786432 | tf_op jit(solution)/shard_map/all_to_all | solution.py:37
  42.5 7.2 all-to-all-start.1
  49.9 1.6 collective-permute-start
  51.5 2.7 collective-permute-start.1
  54.7 2.4 collective-permute-start.3
  57.1 21.0 %all-to-all-done.1 = bf16[6,128,256]{2,0,1:T(8,128)(2,1)S(1)} async-done(((bf16[6,128,256]{2,0,1:T(8,128)(2,1)}), bf16[6,128,256]{2,0,1:T(8,128)(2,1)S(1)}, u32[]{:S(2)}, u32[]{:S(2)}) %all-to-all-start.1) | async-done | bytes 393248 | tf_op jit(solution)/shard_map/all_to_all | solution.py:41
  78.2 1.1 copy.15
  79.3 1.3 fusion.13
  80.6 1.3 fusion.12
  82.9 1.0 multiply_convert_fusion
  84.7 1.6 copy.19
  86.3 2.5 reshape.108
  88.9 1.0 copy-done.4
  89.9 0.7 slice_bitcast_fusion.3
  90.6 0.9 collective-permute-start.7
  91.7 1.8 collective-permute-start.11
  93.5 1.4 collective-permute-start.6
  94.9 2.0 collective-permute-start.8
  97.2 1.2 fusion.39
  98.4 1.2 fusion.40
  100.2 4.8 collective-permute-done.6
  105.5 1.2 fusion.43
  106.8 1.0 collective-permute-start.4
  107.7 1.2 fusion.44
  108.9 8.4 collective-permute-done.10
  117.3 1.2 fusion.45
  118.5 1.9 convert_element_type.63
  120.4 801.2 %reduce-scatter.15.cloned.1.call-done = f32[24,128]{1,0:T(8,128)} async-done(((f32[3072,128]{1,0:T(8,128)}), f32[24,128]{1,0:T(8,128)}) %reduce-scatter.15.cloned.1.call-update) | async-done | bytes 12304
  921.6 0.7 convert_element_type.55
  922.3 337.9 %all_gather.3 = bf16[3072,128]{1,0:T(8,128)(2,1)S(1)} all-gather(bf16[24,128]{1,0:T(8,128)(2,1)S(1)} %convert_element_type.55), channel_id=1, replica_groups=mesh['hid'=128,'seq'=2] {'hid'}, dimensions={0}, use_global_device_ids=true | all-gather | bytes 792576 | tf_op jit(solution)/shard_map/all_gather | solution.py:23
  1260.9 2.1 convolution_add_fusion.1
  1263.0 1.0 fusion.14
  1264.0 1.7 copy.22
  1265.7 2.8 fusion.8
  1268.5 1.9 all_to_all.64
  1270.4 16.0 %all-to-all-start.3 = ((bf16[128,6,256]{2,1,0:T(8,128)(2,1)}), bf16[128,6,256]{2,1,0:T(8,128)(2,1)S(1)}, u32[]{:S(2)}, u32[]{:S(2)}) async-start(bf16[128,6,256]{2,1,0:T(8,128)(2,1)} %all_to_all.64), calls=%async_computation.3 | async-start | bytes 1048576 | tf_op jit(solution)/shard_map/all_to_all | solution.py:78
  1286.5 1.0 fusion.15
  1287.8 1.3 convolution_add_fusion.3
  1289.2 1.3 fusion.7
  1290.5 0.9 all_to_all.60
  1291.4 0.9 copy.23
  1293.1 11.3 reduce-scatter.11.cloned.1.call-done
  1304.4 1.5 convert_element_type.67
  1305.9 13.8 %all-to-all-start.2 = ((bf16[128,6,256]{2,1,0:T(8,128)(2,1)}), bf16[128,6,256]{2,1,0:T(8,128)(2,1)S(1)}, u32[]{:S(2)}, u32[]{:S(2)}) async-start(bf16[128,6,256]{2,1,0:T(8,128)(2,1)} %all_to_all.60), calls=%async_computation.2 | async-start | bytes 1048576 | tf_op jit(solution)/shard_map/all_to_all | solution.py:52
  1319.8 1.5 fusion.18
  1321.3 18.0 %all-to-all-done.2 = bf16[128,6,256]{2,1,0:T(8,128)(2,1)S(1)} async-done(((bf16[128,6,256]{2,1,0:T(8,128)(2,1)}), bf16[128,6,256]{2,1,0:T(8,128)(2,1)S(1)}, u32[]{:S(2)}, u32[]{:S(2)}) %all-to-all-start.2) | async-done | bytes 393248 | tf_op jit(solution)/shard_map/all_to_all | solution.py:52
  1339.3 0.8 copy.33
  (56 shorter events, 6.3 us)
Async XLA Ops:
  7.2 77.1 %copy-start = (bf16[256,256]{1,0:T(8,128)(2,1)S(1)}, bf16[256,256]{1,0:T(8,128)(2,1)}, u32[]{:S(2)}) copy-start(bf16[256,256]{1,0:T(8,128)(2,1)} %param.7) | copy-start | bytes 393220
  42.5 35.5 %all-to-all-start.1 = ((bf16[6,128,256]{2,0,1:T(8,128)(2,1)}), bf16[6,128,256]{2,0,1:T(8,128)(2,1)S(1)}, u32[]{:S(2)}, u32[]{:S(2)}) async-start(bf16[6,128,256]{2,0,1:T(8,128)(2,1)} %bitcast.3), calls=%async_computation.1 | async-start | bytes 1048576 | tf_op jit(solution)/shard_map/all_to_all | solution.py:41
  49.7 68.8 %reduce-scatter.9.cloned.1.call-start = ((), (), s32[]{:S(2)}) async-start(), calls=%async_computation.8 | async-start | bytes 983040 | tf_op jit(solution)/shard_map/reduce_scatter | solution.py:68
  49.9 30.6 %collective-permute-start = (bf16[768,256]{1,0:T(8,128)(2,1)S(1)}, bf16[768,256]{1,0:T(8,128)(2,1)}, u32[]{:S(2)}, u32[]{:S(2)}) collective-permute-start(bf16[768,256]{1,0:T(8,128)(2,1)S(1)} %all_to_all.55), channel_id=1, source_target_pairs={{0,2},{2,0},{4,6},{6,4},{8,10},{10,8},{12,14},{14,12},{16,18},{18,... | collective-permute-start | bytes 1179656 | tf_op jit(solution)/shard_map/ppermute | solution.py:11
  51.5 30.4 %collective-permute-start.1 = (bf16[768,256]{1,0:T(8,128)(2,1)S(1)}, bf16[768,256]{1,0:T(8,128)(2,1)S(1)}, u32[]{:S(2)}, u32[]{:S(2)}) collective-permute-start(bf16[768,256]{1,0:T(8,128)(2,1)S(1)} %all_to_all.55), channel_id=1, source_target_pairs={{0,4},{2,6},{4,0},{6,2},{8,12},{10,14},{12,8},{14,10},{16,20},{18,... | collective-permute-start | bytes 1179656 | tf_op jit(solution)/shard_map/ppermute | solution.py:11
  54.2 28.1 %collective-permute-start.2 = (bf16[768,256]{1,0:T(8,128)(2,1)S(1)}, bf16[768,256]{1,0:T(8,128)(2,1)S(1)}, u32[]{:S(2)}, u32[]{:S(2)}) collective-permute-start(bf16[768,256]{1,0:T(8,128)(2,1)S(1)} %all_to_all.55), channel_id=1, source_target_pairs={{0,8},{2,10},{4,12},{6,14},{8,0},{10,2},{12,4},{14,6},{16,24},{18,... | collective-permute-start | bytes 1179656 | tf_op jit(solution)/shard_map/ppermute | solution.py:11
  54.7 27.8 %collective-permute-start.3 = (bf16[768,256]{1,0:T(8,128)(2,1)S(1)}, bf16[768,256]{1,0:T(8,128)(2,1)S(1)}, u32[]{:S(2)}, u32[]{:S(2)}) collective-permute-start(bf16[768,256]{1,0:T(8,128)(2,1)S(1)} %all_to_all.55), channel_id=1, source_target_pairs={{0,16},{2,18},{4,20},{6,22},{8,24},{10,26},{12,28},{14,30},{16,0},... | collective-permute-start | bytes 1179656 | tf_op jit(solution)/shard_map/ppermute | solution.py:11
  82.6 1.3 copy-start.6
  82.9 1.1 copy-start.8
  83.9 837.7 %reduce-scatter.15.cloned.1.call-start = ((), (), s32[]{:S(2)}) async-start(), calls=%async_computation.11 | async-start | bytes 1585152
  88.8 1.1 copy-start.4
  88.8 1202.6 %reduce-scatter.13.cloned.1.call-start = ((), (), s32[]{:S(2)}) async-start(), calls=%async_computation.10 | async-start | bytes 196608
  90.6 9.0 collective-permute-start.7
  91.4 15.3 %collective-permute-start.9 = (bf16[256,256]{1,0:T(8,128)(2,1)S(1)}, bf16[256,256]{1,0:T(8,128)(2,1)S(1)}, u32[]{:S(2)}, u32[]{:S(2)}) collective-permute-start(bf16[256,256]{1,0:T(8,128)(2,1)S(1)} %get-tuple-element.8), channel_id=1, source_target_pairs={{0,8},{2,10},{4,12},{6,14},{8,0},{10,2},{12,4},{14,6},{16,24},{18,... | collective-permute-start | bytes 393224 | tf_op jit(solution)/shard_map/ppermute | solution.py:11
  91.7 6.7 copy-start.7
  91.7 17.2 %collective-permute-start.11 = (bf16[256,256]{1,0:T(8,128)(2,1)S(1)}, bf16[256,256]{1,0:T(8,128)(2,1)S(1)}, u32[]{:S(2)}, u32[]{:S(2)}) collective-permute-start(bf16[256,256]{1,0:T(8,128)(2,1)S(1)} %get-tuple-element.7), channel_id=1, source_target_pairs={{0,16},{2,18},{4,20},{6,22},{8,24},{10,26},{12,28},{14,30},{16,0},... | collective-permute-start | bytes 393224 | tf_op jit(solution)/shard_map/ppermute | solution.py:11
  93.5 11.5 collective-permute-start.6
  94.9 12.8 collective-permute-start.8
  99.6 1166.1 %collective-permute-start.5 = (bf16[256,256]{1,0:T(8,128)(2,1)}, bf16[256,256]{1,0:T(8,128)(2,1)S(1)}, u32[]{:S(2)}, u32[]{:S(2)}) collective-permute-start(bf16[256,256]{1,0:T(8,128)(2,1)} %get-tuple-element.5), channel_id=1, source_target_pairs={{0,2},{2,0},{4,6},{6,4},{8,10},{10,8},{12,14},{14,12},{16,18},{18,... | collective-permute-start | bytes 393224 | tf_op jit(solution)/shard_map/ppermute | solution.py:11
  105.0 12.3 collective-permute-start.10
  106.8 1158.9 %collective-permute-start.4 = (bf16[768,256]{1,0:T(8,128)(2,1)S(1)}, bf16[768,256]{1,0:T(8,128)(2,1)}, u32[]{:S(2)}, u32[]{:S(2)}) collective-permute-start(bf16[768,256]{1,0:T(8,128)(2,1)S(1)} %all_to_all.59), channel_id=1, source_target_pairs={{0,2},{2,0},{4,6},{6,4},{8,10},{10,8},{12,14},{14,12},{16,18},{18,... | collective-permute-start | bytes 1179656 | tf_op jit(solution)/shard_map/ppermute | solution.py:11
  1263.0 2.7 copy-start.3
  1270.4 35.5 %all-to-all-start.3 = ((bf16[128,6,256]{2,1,0:T(8,128)(2,1)}), bf16[128,6,256]{2,1,0:T(8,128)(2,1)S(1)}, u32[]{:S(2)}, u32[]{:S(2)}) async-start(bf16[128,6,256]{2,1,0:T(8,128)(2,1)} %all_to_all.64), calls=%async_computation.3 | async-start | bytes 1048576 | tf_op jit(solution)/shard_map/all_to_all | solution.py:78
  1286.4 17.9 %reduce-scatter.11.cloned.1.call-start = ((), (), s32[]{:S(2)}) async-start(), calls=%async_computation.9 | async-start | bytes 196608 | tf_op jit(solution)/shard_map/reduce_scatter | solution.py:74
  1287.7 1.3 copy-start.1
  1287.8 1.4 copy-start.2
  1305.9 13.9 %copy-start.5 = (bf16[6,32768]{1,0:T(8,128)(2,1)S(1)}, bf16[6,32768]{1,0:T(8,128)(2,1)}, u32[]{:S(2)}) copy-start(bf16[6,32768]{1,0:T(8,128)(2,1)} %param.5) | copy-start | bytes 1179652
  1305.9 33.4 %all-to-all-start.2 = ((bf16[128,6,256]{2,1,0:T(8,128)(2,1)}), bf16[128,6,256]{2,1,0:T(8,128)(2,1)S(1)}, u32[]{:S(2)}, u32[]{:S(2)}) async-start(bf16[128,6,256]{2,1,0:T(8,128)(2,1)} %all_to_all.60), calls=%async_computation.2 | async-start | bytes 1048576 | tf_op jit(solution)/shard_map/all_to_all | solution.py:52
Sparse Core Ops, SparseCore 0:
  84.0 9.1 reduce-scatter.8
  98.7 822.8 reduce-scatter.14
  1265.8 13.9 reduce-scatter.12
  1290.0 14.3 reduce-scatter.10
where the time goes:
time: 1350 us
  waiting for transfers between devices  865 us (64%)
  blocking collectives  372 us (28%)
  starting transfers between devices  52.9 us (4%)
  matrix products  20.3 us (2%)
  between operations  14.1 us (1%)
  local copies, waits for them, and re-layouts  14 us (1%)
    unnamed x6, waiting for transfers between devices  801 us
    all_gather x1, blocking collectives, reduce_latents(): full = lax.all_gather(part.astype(jnp.bfloat16), 'hid', axis=0, tiled=True)  338 us
    all_to_all x1, blocking collectives, on_device(): lax.all_to_all(act_tok, 'hid', split_axis=1, concat_axis=0, tiled=True)  33.9 us
  transfers between devices with their start and end apart: 19, of which 6 were waited for; matrix products, arithmetic and copies ran while one was open for 3% of the time, Pallas kernels for 0%

commit v1 on v0

--- a/solution.py
+++ b/solution.py
@@ -5,6 +5,11 @@
 from jax.sharding import PartitionSpec as P
 
 LEVELS = 4
+
+
+def swapped_in(x, name, dim):
+    repeated = jnp.stack([x] * lax.axis_size(name))
+    return jnp.concatenate(lax.all_to_all(repeated, name, 0, 0), axis=dim)
 
 
 def swapped(x, axis, stride):
@@ -20,7 +25,7 @@
     rows, wide = both.shape
     flat = both.reshape(rows * wide // 128, 128)
     part = lax.psum_scatter(flat, "hid", scatter_dimension=0, tiled=True)
-    full = lax.all_gather(part.astype(jnp.bfloat16), "hid", axis=0, tiled=True)
+    full = swapped_in(part.astype(jnp.bfloat16), "hid", 0)
     full = full.reshape(rows, wide)
     return (full[:, : wide // 2], full[:, wide // 2 :])
 

time: 1350 us -> 1030 us (0.76)
  blocking collectives: 372 us -> 0 us
  starting transfers between devices: 52.9 us -> 81 us
  waiting for transfers between devices: 865 us -> 880 us
    all_gather x1 -> x0, blocking collectives: 338 us -> none  [reduce_latents(): full = lax.all_gather(part.astype(jnp.bfloat16), 'hid', axis=0, tiled=True)]
    all_to_all x1 -> x0, blocking collectives: 33.9 us -> none  [on_device(): lax.all_to_all(act_tok, 'hid', split_axis=1, concat_axis=0, tiled=True)]
    all_to_all x0 -> x2, starting transfers between devices: none -> 18.9 us  [the longest x1 11.5 us: swapped_in(): return jnp.concatenate(lax.all_to_all(repeated, name, 0, 0), axis=dim)]
    ppermute x12, waiting for transfers between devices: 13.2 us -> 31.5 us  [swapped(): lax.ppermute(x, axis, [(i, i ^ 1 << stride) for i in range(lax.axis_size(...]
    unnamed x6, waiting for transfers between devices: 801 us -> 783 us
    all_to_all x0 -> x2, waiting for transfers between devices: none -> 17.8 us  [the longest x1 17.8 us: on_device(): lax.all_to_all(act_tok, 'hid', split_axis=1, concat_axis=0, tiled=True)]
  transfers between devices with their start and end apart: 19 -> 21, of which waited for: 6 -> 9; matrix products, arithmetic and copies ran while one was open for 3% -> 4% of each run, Pallas kernels for 0% -> 0%
where the time goes in v1:
time: 1030 us; the launch traced here: 1020 us
  waiting for transfers between devices  880 us (85%)
  starting transfers between devices  81 us (8%)
  matrix products  24.7 us (2%)
  between operations  16 us (2%)
  local copies, waits for them, and re-layouts  13.4 us (1%)
    unnamed x6, waiting for transfers between devices  783 us
    ppermute x12, waiting for transfers between devices, swapped(): lax.ppermute(x, axis, [(i, i ^ 1 << stride) for i in range(lax.axis_size(...  31.5 us
  transfers between devices with their start and end apart: 21, of which 9 were waited for; matrix products, arithmetic and copies ran while one was open for 4% of the time, Pallas kernels for 0%

profile of v1, /device:TPU:32, one launch (start us, length us, event | category | flops | bytes accessed | tf_op | source)
XLA Modules:
  0.0 1024.8 jit_solution(8134420153605740223)
XLA Ops:
  8.0 15.1 %all-to-all-start.1 = ((bf16[6,128,256]{2,0,1:T(8,128)(2,1)}), bf16[6,128,256]{2,0,1:T(8,128)(2,1)S(1)}, u32[]{:S(2)}, u32[]{:S(2)}) async-start(bf16[6,128,256]{2,0,1:T(8,128)(2,1)} %bitcast.92), calls=%async_computation.1 | async-start | bytes 1048576 | tf_op jit(solution)/shard_map/all_to_all | solution.py:46
  23.2 1.2 fusion.22
  24.3 18.0 %all-to-all-done.1 = bf16[6,128,256]{2,0,1:T(8,128)(2,1)S(1)} async-done(((bf16[6,128,256]{2,0,1:T(8,128)(2,1)}), bf16[6,128,256]{2,0,1:T(8,128)(2,1)S(1)}, u32[]{:S(2)}, u32[]{:S(2)}) %all-to-all-start.1) | async-done | bytes 393248 | tf_op jit(solution)/shard_map/all_to_all | solution.py:46
  42.3 7.3 all-to-all-start
  49.8 17.8 %all-to-all-done = bf16[6,128,256]{2,0,1:T(8,128)(2,1)S(1)} async-done(((bf16[6,128,256]{2,0,1:T(8,128)(2,1)}), bf16[6,128,256]{2,0,1:T(8,128)(2,1)S(1)}, u32[]{:S(2)}, u32[]{:S(2)}) %all-to-all-start) | async-done | bytes 393248 | tf_op jit(solution)/shard_map/all_to_all | solution.py:42
  68.5 1.6 copy.19
  70.2 2.5 reshape.107
  72.7 1.0 collective-permute-start
  74.5 2.4 collective-permute-start.7
  77.3 2.0 collective-permute-start.11
  79.3 1.8 collective-permute-start.1
  81.1 1.1 copy.15
  82.2 2.0 fusion.13
  84.8 1.2 collective-permute-start.2
  86.0 1.0 fusion.12
  87.0 6.7 collective-permute-done.1
  94.5 1.0 fusion.11
  95.5 1.5 collective-permute-start.6
  97.0 1.0 fusion.10
  98.0 9.8 collective-permute-done.3
  107.8 2.6 collective-permute-start.8
  110.4 1.0 fusion.9
  111.4 783.3 %reduce-scatter.15.cloned.1.call-done = f32[24,128]{1,0:T(8,128)} async-done(((f32[3072,128]{1,0:T(8,128)}), f32[24,128]{1,0:T(8,128)}) %reduce-scatter.15.cloned.1.call-update) | async-done | bytes 12304
  895.4 1.0 stack.14
  896.4 11.5 %all-to-all-start.2 = ((bf16[128,24,128]{2,1,0:T(8,128)(2,1)}), bf16[128,24,128]{2,1,0:T(8,128)(2,1)S(1)}, u32[]{:S(2)}, u32[]{:S(2)}) async-start(bf16[128,24,128]{2,1,0:T(8,128)(2,1)} %stack.14), calls=%async_computation.2 | async-start | bytes 1572864 | tf_op jit(solution)/shard_map/all_to_all | solution.py:12
  908.0 2.3 multiply_convert_fusion
  910.4 1.2 fusion.38
  911.6 1.1 fusion.39
  912.7 1.2 fusion.40
  913.9 1.5 collective-permute-start.5
  915.3 2.4 collective-permute-start.10
  917.7 2.2 fusion.43
  920.5 1.3 fusion.44
  921.8 14.3 %collective-permute-done.10 = bf16[768,256]{1,0:T(8,128)(2,1)S(1)} collective-permute-done((bf16[768,256]{1,0:T(8,128)(2,1)S(1)}, bf16[768,256]{1,0:T(8,128)(2,1)S(1)}, u32[]{:S(2)}, u32[]{:S(2)}) %collective-permute-start.10) | collective-permute-done | bytes 393248 | tf_op jit(solution)/shard_map/ppermute | solution.py:16
  936.2 2.1 fusion.45
  938.2 1.9 convert_element_type.63
  940.9 2.1 convolution_add_fusion.1
  944.1 2.6 fusion.8
  946.7 1.9 all_to_all.68
  948.6 15.0 %all-to-all-start.4 = ((bf16[128,6,256]{2,1,0:T(8,128)(2,1)}), bf16[128,6,256]{2,1,0:T(8,128)(2,1)S(1)}, u32[]{:S(2)}, u32[]{:S(2)}) async-start(bf16[128,6,256]{2,1,0:T(8,128)(2,1)} %all_to_all.68), calls=%async_computation.4 | async-start | bytes 1048576 | tf_op jit(solution)/shard_map/all_to_all | solution.py:83
  963.7 1.0 fusion.15
  965.0 1.3 convolution_add_fusion.3
  966.5 1.2 fusion.7
  970.3 11.1 %reduce-scatter.11.cloned.1.call-done = bf16[128,256]{1,0:T(8,128)(2,1)} async-done(((bf16[256,256]{1,0:T(8,128)(2,1)}), bf16[128,256]{1,0:T(8,128)(2,1)}) %reduce-scatter.11.cloned.1.call-update) | async-done | bytes 65552 | tf_op jit(solution)/shard_map/reduce_scatter | solution.py:79
  981.4 1.5 convert_element_type.67
  982.9 13.8 %all-to-all-start.3 = ((bf16[128,6,256]{2,1,0:T(8,128)(2,1)}), bf16[128,6,256]{2,1,0:T(8,128)(2,1)S(1)}, u32[]{:S(2)}, u32[]{:S(2)}) async-start(bf16[128,6,256]{2,1,0:T(8,128)(2,1)} %all_to_all.64), calls=%async_computation.3 | async-start | bytes 1048576 | tf_op jit(solution)/shard_map/all_to_all | solution.py:57
  996.8 1.5 fusion.18
  998.3 18.1 %all-to-all-done.3 = bf16[128,6,256]{2,1,0:T(8,128)(2,1)S(1)} async-done(((bf16[128,6,256]{2,1,0:T(8,128)(2,1)}), bf16[128,6,256]{2,1,0:T(8,128)(2,1)S(1)}, u32[]{:S(2)}, u32[]{:S(2)}) %all-to-all-start.3) | async-done | bytes 393248 | tf_op jit(solution)/shard_map/all_to_all | solution.py:57
  (69 shorter events, 11.0 us)
Async XLA Ops:
  8.0 60.1 %copy-start = (bf16[256,256]{1,0:T(8,128)(2,1)S(1)}, bf16[256,256]{1,0:T(8,128)(2,1)}, u32[]{:S(2)}) copy-start(bf16[256,256]{1,0:T(8,128)(2,1)} %param.7) | copy-start | bytes 393220
  8.0 15.2 %copy-start.8 = (bf16[6,32768]{1,0:T(8,128)(2,1)S(1)}, bf16[6,32768]{1,0:T(8,128)(2,1)}, u32[]{:S(2)}) copy-start(bf16[6,32768]{1,0:T(8,128)(2,1)} %param.5) | copy-start | bytes 1179652
  8.0 34.3 %all-to-all-start.1 = ((bf16[6,128,256]{2,0,1:T(8,128)(2,1)}), bf16[6,128,256]{2,0,1:T(8,128)(2,1)S(1)}, u32[]{:S(2)}, u32[]{:S(2)}) async-start(bf16[6,128,256]{2,0,1:T(8,128)(2,1)} %bitcast.92), calls=%async_computation.1 | async-start | bytes 1048576 | tf_op jit(solution)/shard_map/all_to_all | solution.py:46
  42.3 25.5 %copy-start.6 = (bf16[6,128,256]{2,0,1:T(8,128)(2,1)}, bf16[6,128,256]{2,0,1:T(8,128)(2,1)S(1)}, u32[]{:S(2)}) copy-start(bf16[6,128,256]{2,0,1:T(8,128)(2,1)S(1)} %all-to-all-done.1) | copy-start | bytes 1179652
  42.3 25.5 %copy-start.12 = (bf16[256,256]{1,0:T(8,128)(2,1)S(1)}, bf16[256,256]{1,0:T(8,128)(2,1)}, u32[]{:S(2)}) copy-start(bf16[256,256]{1,0:T(8,128)(2,1)} %param.8) | copy-start | bytes 393220
  42.3 25.3 %all-to-all-start = ((bf16[6,128,256]{2,0,1:T(8,128)(2,1)}), bf16[6,128,256]{2,0,1:T(8,128)(2,1)S(1)}, u32[]{:S(2)}, u32[]{:S(2)}) async-start(bf16[6,128,256]{2,0,1:T(8,128)(2,1)} %bitcast), calls=%async_computation | async-start | bytes 1048576 | tf_op jit(solution)/shard_map/all_to_all | solution.py:42
  49.6 845.1 %reduce-scatter.15.cloned.1.call-start = ((), (), s32[]{:S(2)}) async-start(), calls=%async_computation.12 | async-start | bytes 1585152
  72.7 1.1 copy-start.5
  72.7 9.5 copy-start.7
  72.7 12.1 %collective-permute-start = (bf16[768,256]{1,0:T(8,128)(2,1)S(1)}, bf16[768,256]{1,0:T(8,128)(2,1)S(1)}, u32[]{:S(2)}, u32[]{:S(2)}) collective-permute-start(bf16[768,256]{1,0:T(8,128)(2,1)S(1)} %all_to_all.58), channel_id=1, source_target_pairs={{0,2},{2,0},{4,6},{6,4},{8,10},{10,8},{12,14},{14,12},{16,18},{18,... | collective-permute-start | bytes 1179656 | tf_op jit(solution)/shard_map/ppermute | solution.py:16
  74.5 839.3 %collective-permute-start.7 = (bf16[256,256]{1,0:T(8,128)(2,1)}, bf16[256,256]{1,0:T(8,128)(2,1)}, u32[]{:S(2)}, u32[]{:S(2)}) collective-permute-start(bf16[256,256]{1,0:T(8,128)(2,1)} %get-tuple-element.6), channel_id=1, source_target_pairs={{0,4},{2,6},{4,0},{6,2},{8,12},{10,14},{12,8},{14,10},{16,20},{18,... | collective-permute-start | bytes 393224 | tf_op jit(solution)/shard_map/ppermute | solution.py:16
  76.9 843.0 %collective-permute-start.9 = (bf16[256,256]{1,0:T(8,128)(2,1)}, bf16[256,256]{1,0:T(8,128)(2,1)}, u32[]{:S(2)}, u32[]{:S(2)}) collective-permute-start(bf16[256,256]{1,0:T(8,128)(2,1)} %get-tuple-element.8), channel_id=1, source_target_pairs={{0,8},{2,10},{4,12},{6,14},{8,0},{10,2},{12,4},{14,6},{16,24},{18,... | collective-permute-start | bytes 393224 | tf_op jit(solution)/shard_map/ppermute | solution.py:16
  77.3 844.5 %collective-permute-start.11 = (bf16[256,256]{1,0:T(8,128)(2,1)}, bf16[256,256]{1,0:T(8,128)(2,1)}, u32[]{:S(2)}, u32[]{:S(2)}) collective-permute-start(bf16[256,256]{1,0:T(8,128)(2,1)} %get-tuple-element.7), channel_id=1, source_target_pairs={{0,16},{2,18},{4,20},{6,22},{8,24},{10,26},{12,28},{14,30},{16,0},... | collective-permute-start | bytes 393224 | tf_op jit(solution)/shard_map/ppermute | solution.py:16
  79.3 14.3 %collective-permute-start.1 = (bf16[768,256]{1,0:T(8,128)(2,1)S(1)}, bf16[768,256]{1,0:T(8,128)(2,1)S(1)}, u32[]{:S(2)}, u32[]{:S(2)}) collective-permute-start(bf16[768,256]{1,0:T(8,128)(2,1)S(1)} %all_to_all.58), channel_id=1, source_target_pairs={{0,4},{2,6},{4,0},{6,2},{8,12},{10,14},{12,8},{14,10},{16,20},{18,... | collective-permute-start | bytes 1179656 | tf_op jit(solution)/shard_map/ppermute | solution.py:16
  84.8 13.2 %copy-start.10 = (bf16[768,256]{1,0:T(8,128)(2,1)}, bf16[768,256]{1,0:T(8,128)(2,1)S(1)}, u32[]{:S(2)}) copy-start(bf16[768,256]{1,0:T(8,128)(2,1)S(1)} %collective-permute-done) | copy-start | bytes 1179652
  84.8 10.7 %collective-permute-start.2 = (bf16[768,256]{1,0:T(8,128)(2,1)S(1)}, bf16[768,256]{1,0:T(8,128)(2,1)S(1)}, u32[]{:S(2)}, u32[]{:S(2)}) collective-permute-start(bf16[768,256]{1,0:T(8,128)(2,1)S(1)} %all_to_all.58), channel_id=1, source_target_pairs={{0,8},{2,10},{4,12},{6,14},{8,0},{10,2},{12,4},{14,6},{16,24},{18,... | collective-permute-start | bytes 1179656 | tf_op jit(solution)/shard_map/ppermute | solution.py:16
  93.7 14.2 %collective-permute-start.3 = (bf16[768,256]{1,0:T(8,128)(2,1)S(1)}, bf16[768,256]{1,0:T(8,128)(2,1)S(1)}, u32[]{:S(2)}, u32[]{:S(2)}) collective-permute-start(bf16[768,256]{1,0:T(8,128)(2,1)S(1)} %all_to_all.58), channel_id=1, source_target_pairs={{0,16},{2,18},{4,20},{6,22},{8,24},{10,26},{12,28},{14,30},{16,0},... | collective-permute-start | bytes 1179656 | tf_op jit(solution)/shard_map/ppermute | solution.py:16
  95.5 819.9 %collective-permute-start.6 = (bf16[768,256]{1,0:T(8,128)(2,1)S(1)}, bf16[768,256]{1,0:T(8,128)(2,1)}, u32[]{:S(2)}, u32[]{:S(2)}) collective-permute-start(bf16[768,256]{1,0:T(8,128)(2,1)S(1)} %all_to_all.62), channel_id=1, source_target_pairs={{0,4},{2,6},{4,0},{6,2},{8,12},{10,14},{12,8},{14,10},{16,20},{18,... | collective-permute-start | bytes 1179656 | tf_op jit(solution)/shard_map/ppermute | solution.py:16
  107.8 812.6 %collective-permute-start.8 = (bf16[768,256]{1,0:T(8,128)(2,1)S(1)}, bf16[768,256]{1,0:T(8,128)(2,1)}, u32[]{:S(2)}, u32[]{:S(2)}) collective-permute-start(bf16[768,256]{1,0:T(8,128)(2,1)S(1)} %all_to_all.62), channel_id=1, source_target_pairs={{0,8},{2,10},{4,12},{6,14},{8,0},{10,2},{12,4},{14,6},{16,24},{18,... | collective-permute-start | bytes 1179656 | tf_op jit(solution)/shard_map/ppermute | solution.py:16
  896.4 43.7 %all-to-all-start.2 = ((bf16[128,24,128]{2,1,0:T(8,128)(2,1)}), bf16[128,24,128]{2,1,0:T(8,128)(2,1)S(1)}, u32[]{:S(2)}, u32[]{:S(2)}) async-start(bf16[128,24,128]{2,1,0:T(8,128)(2,1)} %stack.14), calls=%async_computation.2 | async-start | bytes 1572864 | tf_op jit(solution)/shard_map/all_to_all | solution.py:12
  908.0 30.3 %reduce-scatter.9.cloned.1.call-start = ((), (), s32[]{:S(2)}) async-start(), calls=%async_computation.9 | async-start | bytes 983040 | tf_op jit(solution)/shard_map/reduce_scatter | solution.py:73
  910.3 58.3 %reduce-scatter.13.cloned.1.call-start = ((), (), s32[]{:S(2)}) async-start(), calls=%async_computation.11 | async-start | bytes 196608
  913.9 30.2 %collective-permute-start.5 = (bf16[256,256]{1,0:T(8,128)(2,1)}, bf16[256,256]{1,0:T(8,128)(2,1)S(1)}, u32[]{:S(2)}, u32[]{:S(2)}) collective-permute-start(bf16[256,256]{1,0:T(8,128)(2,1)} %get-tuple-element.5), channel_id=1, source_target_pairs={{0,2},{2,0},{4,6},{6,4},{8,10},{10,8},{12,14},{14,12},{16,18},{18,... | collective-permute-start | bytes 393224 | tf_op jit(solution)/shard_map/ppermute | solution.py:16
  915.3 20.8 %collective-permute-start.10 = (bf16[768,256]{1,0:T(8,128)(2,1)S(1)}, bf16[768,256]{1,0:T(8,128)(2,1)S(1)}, u32[]{:S(2)}, u32[]{:S(2)}) collective-permute-start(bf16[768,256]{1,0:T(8,128)(2,1)S(1)} %all_to_all.62), channel_id=1, source_target_pairs={{0,16},{2,18},{4,20},{6,22},{8,24},{10,26},{12,28},{14,30},{16,0},... | collective-permute-start | bytes 1179656 | tf_op jit(solution)/shard_map/ppermute | solution.py:16
  919.9 24.2 %collective-permute-start.4 = (bf16[768,256]{1,0:T(8,128)(2,1)S(1)}, bf16[768,256]{1,0:T(8,128)(2,1)}, u32[]{:S(2)}, u32[]{:S(2)}) collective-permute-start(bf16[768,256]{1,0:T(8,128)(2,1)S(1)} %all_to_all.62), channel_id=1, source_target_pairs={{0,2},{2,0},{4,6},{6,4},{8,10},{10,8},{12,14},{14,12},{16,18},{18,... | collective-permute-start | bytes 1179656 | tf_op jit(solution)/shard_map/ppermute | solution.py:16
  943.0 1.1 copy-start.4
  948.6 16.1 %copy-start.13 = (bf16[256,256]{1,0:T(8,128)(2,1)S(1)}, bf16[256,256]{1,0:T(8,128)(2,1)}, u32[]{:S(2)}) copy-start(bf16[256,256]{1,0:T(8,128)(2,1)} %param.8) | copy-start | bytes 393220
  948.6 34.3 %all-to-all-start.4 = ((bf16[128,6,256]{2,1,0:T(8,128)(2,1)}), bf16[128,6,256]{2,1,0:T(8,128)(2,1)S(1)}, u32[]{:S(2)}, u32[]{:S(2)}) async-start(bf16[128,6,256]{2,1,0:T(8,128)(2,1)} %all_to_all.68), calls=%async_computation.4 | async-start | bytes 1048576 | tf_op jit(solution)/shard_map/all_to_all | solution.py:83
  963.6 17.7 %reduce-scatter.11.cloned.1.call-start = ((), (), s32[]{:S(2)}) async-start(), calls=%async_computation.10 | async-start | bytes 196608 | tf_op jit(solution)/shard_map/reduce_scatter | solution.py:79
  964.7 1.6 copy-start.3
  964.9 1.4 copy-start.1
  965.0 1.5 copy-start.2
  965.0 1.6 copy-start.11
  982.9 13.9 %copy-start.9 = (bf16[6,32768]{1,0:T(8,128)(2,1)S(1)}, bf16[6,32768]{1,0:T(8,128)(2,1)}, u32[]{:S(2)}) copy-start(bf16[6,32768]{1,0:T(8,128)(2,1)} %param.5) | copy-start | bytes 1179652
  982.9 33.5 %all-to-all-start.3 = ((bf16[128,6,256]{2,1,0:T(8,128)(2,1)}), bf16[128,6,256]{2,1,0:T(8,128)(2,1)S(1)}, u32[]{:S(2)}, u32[]{:S(2)}) async-start(bf16[128,6,256]{2,1,0:T(8,128)(2,1)} %all_to_all.64), calls=%async_computation.3 | async-start | bytes 1048576 | tf_op jit(solution)/shard_map/all_to_all | solution.py:57
Sparse Core Ops, SparseCore 0:
  72.8 821.8 reduce-scatter.14
Sparse Core Ops, SparseCore 1:
  911.5 14.6 reduce-scatter.8
  944.2 15.2 reduce-scatter.12
  967.1 14.2 reduce-scatter.10
